TPU v7x, 32 devices: a whole 2x2x4 slice. The times are simulated.
32 devices in a mesh: row: 8 (over y, x, core), col: 4 (over z).
Axes of the slice: x: 2, y: 2, z: 4, core: 2. Of those that a mesh axis runs over, the one named last changes fastest.
Arguments:
- velocity: float32 [3, 2, 128, 256, 256], P(None, None, 'row', 'col'), may hold values from -7.5 to 7.5
- accumulator: float32 [3, 2, 128, 256, 256], P(None, None, 'row', 'col'), may hold values from -6 to 6
- remesh_flag: int32 [128], P('row'), may hold values 0 or 1
- remesh_shift: int32 [128], P('row'), may hold values from -128 to 127
- viscosity: float32 [1], replicated, may hold values from 0.0003 to 0.0015
- shear: float32 [1], replicated, may hold values from 8 to 20
- clock: float32 [1], replicated, may hold values from 0 to 0.05
- step: float32 [1], replicated, may hold values from 0.004 to 0.01
Outputs:
- new_velocity: float32 [3, 2, 128, 256, 256], P(None, None, 'row', 'col')
- new_accumulator: float32 [3, 2, 128, 256, 256], P(None, None, 'row', 'col')
- spectra: float32 [2, 128], P(None, 'row')
All inputs are finite; a program needn't handle non-finite values. No bound on the sum of `remesh_flag` on one device may be relied on, other than what follows from the above.
Results may differ from a plain program's by a relative error of at most 0.0001.
Values sent between devices are 32-bit elements; how exact they have to be, the bound alone decides.
A program may use at most 192 MiB of HBM per device.

v0:
```python
import math

import jax
import jax.numpy as jnp
from jax import lax
from jax.sharding import PartitionSpec as P

NX = 256
NY = 256
NZ = 256


def signed_index(positions, period):
    return jnp.where(2 * positions < period, positions, positions - period)


def roll_rows(field, amounts):

    def shift_row(row_data, amount_one):
        return jnp.roll(row_data, -amount_one, axis=-1)

    return jax.vmap(shift_row, in_axes=(2, 0), out_axes=2)(field, amounts)


def dft_tables(period):
    positions = jnp.arange(period, dtype=jnp.int32)
    product = positions[:, None] * positions[None, :] % period
    angles = product.astype(jnp.float32) * (2.0 * math.pi / period)
    factor = 1.0 / math.sqrt(period)
    return (jnp.cos(angles) * factor, jnp.sin(angles) * factor)


def product_high(formula, first_arg, second_arg):
    return jnp.einsum(formula, first_arg, second_arg, precision=lax.Precision.HIGHEST)


def rotate(left_side, right_side, output, real_part, imag_part, cosine_table, sine_table, backward):
    stacked = jnp.stack([real_part, imag_part])
    if backward:
        block_table = jnp.stack(
            [jnp.stack([cosine_table, sine_table]), jnp.stack([-sine_table, cosine_table])]
        )
    else:
        block_table = jnp.stack(
            [jnp.stack([cosine_table, -sine_table]), jnp.stack([sine_table, cosine_table])]
        )
    result = product_high(
        "s" + left_side + ",st" + right_side + "->t" + output, stacked, block_table
    )
    return (result[0], result[1])


def project(real_part, imag_part, wave_vector, inverse_square):
    along_real = (
        wave_vector[0] * real_part[0]
        + wave_vector[1] * real_part[1]
        + wave_vector[2] * real_part[2]
    ) * inverse_square
    along_imag = (
        wave_vector[0] * imag_part[0]
        + wave_vector[1] * imag_part[1]
        + wave_vector[2] * imag_part[2]
    ) * inverse_square
    return (
        jnp.stack([real_part[number] - wave_vector[number] * along_real for number in range(3)]),
        jnp.stack([imag_part[number] - wave_vector[number] * along_imag for number in range(3)]),
    )


def cross_product(first_one, second_one):
    return jnp.stack(
        [
            first_one[1] * second_one[2] - first_one[2] * second_one[1],
            first_one[2] * second_one[0] - first_one[0] * second_one[2],
            first_one[0] * second_one[1] - first_one[1] * second_one[0],
        ]
    )


def to_physical(real_part, imag_part, tables_all):
    (cos_y, sin_y), (cos_x, sin_x), (cos_z, sin_z) = tables_all
    row_count = lax.axis_size("row")
    col_count = lax.axis_size("col")
    fields, width_x, width_z, full_y = real_part.shape
    block_y = full_y // row_count
    half_x = width_x * row_count
    full_x = cos_x.shape[0]
    block_x = full_x // col_count
    full_z = width_z * col_count
    shape_y = (full_y, row_count, block_y)
    first_real, first_imag = rotate(
        "fabc",
        "cpq",
        "fpabq",
        real_part,
        imag_part,
        cos_y.reshape(shape_y),
        sin_y.reshape(shape_y),
        True,
    )
    flat_shape = (fields, row_count, width_x, width_z * block_y)
    second_real, second_imag = (
        lax.all_to_all(
            first_real.reshape(flat_shape), "row", split_axis=1, concat_axis=2, tiled=True
        ),
        lax.all_to_all(
            first_imag.reshape(flat_shape), "row", split_axis=1, concat_axis=2, tiled=True
        ),
    )
    deep_shape = (fields, half_x, width_z, block_y)
    weights = jnp.where(jnp.arange(half_x) == 0, 1.0, 2.0).astype(jnp.float32)[:, None]
    shape_x = (half_x, col_count, block_x)
    cos_half = (weights * cos_x[:half_x]).reshape(shape_x)
    sin_half = (weights * sin_x[:half_x]).reshape(shape_x)
    third_real, third_imag = rotate(
        "fkzy",
        "kpq",
        "fpzyq",
        second_real.reshape(deep_shape),
        second_imag.reshape(deep_shape),
        cos_half,
        sin_half,
        True,
    )
    flat_shape = (fields, col_count, 1, width_z * block_y * block_x)
    fourth_real, fourth_imag = (
        lax.all_to_all(
            third_real.reshape(flat_shape), "col", split_axis=1, concat_axis=2, tiled=True
        ),
        lax.all_to_all(
            third_imag.reshape(flat_shape), "col", split_axis=1, concat_axis=2, tiled=True
        ),
    )
    deep_shape = (fields, col_count, width_z, block_y, block_x)
    shape_z = (col_count, width_z, full_z)
    stacked = jnp.stack([fourth_real.reshape(deep_shape), fourth_imag.reshape(deep_shape)])
    z_table = jnp.stack([cos_z.reshape(shape_z), -sin_z.reshape(shape_z)])
    return product_high("sfpkyq,spkn->fyqn", stacked, z_table)


def to_spectral(physical, tables_all, half_x):
    (cos_y, sin_y), (cos_x, sin_x), (cos_z, sin_z) = tables_all
    row_count = lax.axis_size("row")
    col_count = lax.axis_size("col")
    fields, block_y, block_x, full_z = physical.shape
    width_z = full_z // col_count
    width_x = half_x // row_count
    full_y = block_y * row_count
    shape_z = (full_z, col_count, width_z)
    z_table = jnp.stack([cos_z.reshape(shape_z), -sin_z.reshape(shape_z)])
    first_both = product_high("fyqn,tnpk->tfpkyq", physical, z_table)
    first_real, first_imag = (first_both[0], first_both[1])
    flat_shape = (fields, col_count, 1, width_z * block_y * block_x)
    second_real, second_imag = (
        lax.all_to_all(
            first_real.reshape(flat_shape), "col", split_axis=1, concat_axis=2, tiled=True
        ),
        lax.all_to_all(
            first_imag.reshape(flat_shape), "col", split_axis=1, concat_axis=2, tiled=True
        ),
    )
    deep_shape = (fields, col_count, width_z, block_y, block_x)
    shape_x = (col_count, block_x, row_count, width_x)
    third_real, third_imag = rotate(
        "fpkyq",
        "pqmr",
        "fmrky",
        second_real.reshape(deep_shape),
        second_imag.reshape(deep_shape),
        cos_x[:, :half_x].reshape(shape_x),
        sin_x[:, :half_x].reshape(shape_x),
        False,
    )
    flat_shape = (fields, row_count, 1, width_x * width_z * block_y)
    fourth_real, fourth_imag = (
        lax.all_to_all(
            third_real.reshape(flat_shape), "row", split_axis=1, concat_axis=2, tiled=True
        ),
        lax.all_to_all(
            third_imag.reshape(flat_shape), "row", split_axis=1, concat_axis=2, tiled=True
        ),
    )
    deep_shape = (fields, row_count, width_x, width_z, block_y)
    shape_y = (row_count, block_y, full_y)
    return rotate(
        "fparq",
        "pqn",
        "farn",
        fourth_real.reshape(deep_shape),
        fourth_imag.reshape(deep_shape),
        cos_y.reshape(shape_y),
        sin_y.reshape(shape_y),
        False,
    )


def many_physical(real_part, imag_part, tables_all):
    return jnp.concatenate(
        [
            to_physical(real_part[number : number + 1], imag_part[number : number + 1], tables_all)
            for number in range(real_part.shape[0])
        ]
    )


def many_spectral(physical, tables_all, half_x):
    result_list = [
        to_spectral(physical[number : number + 1], tables_all, half_x)
        for number in range(physical.shape[0])
    ]
    return (
        jnp.concatenate([entry[0] for entry in result_list]),
        jnp.concatenate([entry[1] for entry in result_list]),
    )


def body(velocity, accumulator, remesh_flag, remesh_shift, viscosity, shear, clock, step):
    width_x = velocity.shape[2]
    width_z = velocity.shape[3]
    full_y = velocity.shape[4]
    half_x = width_x * lax.axis_size("row")
    offset = remesh_flag * remesh_shift
    remeshed = roll_rows(velocity, offset)
    carried = roll_rows(accumulator, offset)
    lattice_x = lax.axis_index("row") * width_x + jnp.arange(width_x, dtype=jnp.int32)
    col_index = lax.axis_index("col") * width_z + jnp.arange(width_z, dtype=jnp.int32)
    lattice_z = signed_index(col_index, NZ)
    lattice_y = signed_index(jnp.arange(full_y, dtype=jnp.int32), NY)
    wave_x = lattice_x.astype(jnp.float32)[:, None, None]
    wave_z = lattice_z.astype(jnp.float32)[None, :, None]
    wave_y = lattice_y.astype(jnp.float32)[None, None, :] - shear[0] * clock[0] * wave_x
    wave_vector = (wave_x, wave_y, wave_z)
    square_wave = wave_x * wave_x + wave_y * wave_y + wave_z * wave_z
    inverse_square = 1.0 / jnp.maximum(square_wave, 1.0)
    dealias_mask = (
        (3 * lattice_x < NX)[:, None, None]
        & (3 * jnp.abs(lattice_z) < NZ)[None, :, None]
        & (3 * jnp.abs(lattice_y) < NY)[None, None, :]
    ).astype(jnp.float32)
    shear_rate = shear[0]
    viscous_rate = viscosity[0]
    stress_part = jnp.sum(
        remeshed[0, 0] * remeshed[1, 0] + remeshed[0, 1] * remeshed[1, 1], axis=(1, 2)
    )
    energy = jnp.sum(remeshed * remeshed, axis=(0, 1))
    dissipation_part = jnp.sum(square_wave * energy, axis=(1, 2))
    stress_total, dissipation_total = lax.psum((stress_part, dissipation_part), "col")
    solen_real, solen_imag = project(remeshed[:, 0], remeshed[:, 1], wave_vector, inverse_square)
    smooth_real = dealias_mask * solen_real
    smooth_imag = dealias_mask * solen_imag
    tables_all = (dft_tables(NY), dft_tables(NX), dft_tables(NZ))
    vort_real = -cross_product(wave_vector, smooth_imag)
    vort_imag = cross_product(wave_vector, smooth_real)
    both_real = jnp.concatenate([smooth_real, vort_real])
    both_imag = jnp.concatenate([smooth_imag, vort_imag])
    physical = many_physical(both_real, both_imag, tables_all)
    lamb_grid = cross_product(physical[:3], physical[3:])
    modes_real, modes_imag = many_spectral(lamb_grid, tables_all, half_x)
    hat_real = dealias_mask * modes_real
    hat_imag = dealias_mask * modes_imag
    proj_real, proj_imag = project(hat_real, hat_imag, wave_vector, inverse_square)
    coupling = 2.0 * shear_rate * wave_x * inverse_square

    def tendency(projected, state):
        term_list = [
            projected[number]
            + coupling * wave_vector[number] * state[1]
            - viscous_rate * square_wave * state[number]
            for number in range(3)
        ]
        term_list[0] = term_list[0] - shear_rate * state[1]
        return jnp.stack(term_list)

    tendencies = jnp.stack(
        [tendency(proj_real, remeshed[:, 0]), tendency(proj_imag, remeshed[:, 1])], axis=1
    )
    new_accumulator = -5.0 / 9.0 * carried + step[0] * tendencies
    new_velocity = remeshed + 15.0 / 16.0 * new_accumulator
    stress = stress_total / (NY * NZ)
    dissipation = 2.0 * viscous_rate * dissipation_total / (NY * NZ)
    return (new_velocity, new_accumulator, jnp.stack([stress, dissipation]))


def solution(mesh):
    in_specs = (
        P(None, None, "row", "col", None),
        P(None, None, "row", "col", None),
        P("row"),
        P("row"),
        P(),
        P(),
        P(),
        P(),
    )
    out_specs = (
        P(None, None, "row", "col", None),
        P(None, None, "row", "col", None),
        P(None, "row"),
    )
    return jax.shard_map(body, mesh=mesh, in_specs=in_specs, out_specs=out_specs, check_vma=False)
```

profile of v0, /device:TPU:18, one launch (start us, length us, event | category | flops | bytes accessed | tf_op | source)
XLA Modules:
  0.0 1981.3 jit_solution(11979743943588758129)
XLA Ops:
  7.1 11.6 pad_maximum_fusion
  18.7 29.7 %copy.263 = f32[16,3,2,64,512]{3,1,2,0,4:T(4,128)} copy(f32[16,3,2,64,512]{4,3,2,1,0:T(8,128)} %pad_maximum_fusion) | data formatting | bytes 25165824 | tf_op jit(solution)/shard_map/vmap(jit(_roll_dynamic))/concatenate | solution.py:20
  48.4 16.2 gather_fusion
  64.6 14.8 copy.264
  79.4 14.8 copy.444
  432.3 33.5 %all-to-all-done.6 = f32[1,4,1,131072]{3,2,0,1:T(1,128)S(1)} async-done(((f32[1,4,1,131072]{3,2,0,1:T(1,128)}), f32[1,4,1,131072]{3,2,0,1:T(1,128)S(1)}, u32[]{:S(2)}, u32[]{:S(2)}) %all-to-all-start.6) | async-done | bytes 2097184 | tf_op jit(solution)/shard_map/all_to_all | solution.py:127
  543.0 8.9 convolution_bitcast_fusion.1
  589.4 32.8 %all-to-all-done.22 = f32[1,4,1,131072]{3,2,0,1:T(1,128)} async-done(((f32[1,4,1,131072]{3,2,0,1:T(1,128)}), f32[1,4,1,131072]{3,2,0,1:T(1,128)}, u32[]{:S(2)}, u32[]{:S(2)}) %all-to-all-start.22) | async-done | bytes 2097184 | tf_op jit(solution)/shard_map/all_to_all | solution.py:127
  646.7 8.9 convolution_bitcast_fusion.2
  693.2 32.8 %all-to-all-done.14 = f32[1,4,1,131072]{3,2,0,1:T(1,128)} async-done(((f32[1,4,1,131072]{3,2,0,1:T(1,128)}), f32[1,4,1,131072]{3,2,0,1:T(1,128)}, u32[]{:S(2)}, u32[]{:S(2)}) %all-to-all-start.14) | async-done | bytes 2097184 | tf_op jit(solution)/shard_map/all_to_all | solution.py:127
  750.7 8.9 convolution_bitcast_fusion.5
  797.2 32.8 %all-to-all-done.2 = f32[1,4,1,131072]{3,2,0,1:T(1,128)} async-done(((f32[1,4,1,131072]{3,2,0,1:T(1,128)}), f32[1,4,1,131072]{3,2,0,1:T(1,128)}, u32[]{:S(2)}, u32[]{:S(2)}) %all-to-all-start.2) | async-done | bytes 2097184 | tf_op jit(solution)/shard_map/all_to_all | solution.py:127
  854.6 8.9 convolution_bitcast_fusion
  901.0 32.7 %all-to-all-done.26 = f32[1,4,1,131072]{3,2,0,1:T(1,128)} async-done(((f32[1,4,1,131072]{3,2,0,1:T(1,128)}), f32[1,4,1,131072]{3,2,0,1:T(1,128)}, u32[]{:S(2)}, u32[]{:S(2)}) %all-to-all-start.26) | async-done | bytes 2097184 | tf_op jit(solution)/shard_map/all_to_all | solution.py:127
  952.4 32.8 %all-to-all-done.27 = f32[1,4,1,131072]{3,2,0,1:T(1,128)S(1)} async-done(((f32[1,4,1,131072]{3,2,0,1:T(1,128)}), f32[1,4,1,131072]{3,2,0,1:T(1,128)S(1)}, u32[]{:S(2)}, u32[]{:S(2)}) %all-to-all-start.27) | async-done | bytes 2097184 | tf_op jit(solution)/shard_map/all_to_all | solution.py:130
  1132.0 10.1 fusion.15
  1203.5 31.8 %all-to-all-done.32 = f32[1,4,1,131072]{3,2,0,1:T(1,128)} async-done(((f32[1,4,1,131072]{3,2,0,1:T(1,128)}), f32[1,4,1,131072]{3,2,0,1:T(1,128)}, u32[]{:S(2)}, u32[]{:S(2)}) %all-to-all-start.32) | async-done | bytes 2097184 | tf_op jit(solution)/shard_map/all_to_all | solution.py:155
  1322.9 9.9 fusion.3
  1340.4 9.5 fusion.68
  1368.2 9.3 fusion.66
  1390.8 21.4 %all-to-all-done.16 = f32[1,4,1,131072]{3,2,0,1:T(1,128)} async-done(((f32[1,4,1,131072]{3,2,0,1:T(1,128)}), f32[1,4,1,131072]{3,2,0,1:T(1,128)}, u32[]{:S(2)}, u32[]{:S(2)}) %all-to-all-start.16) | async-done | bytes 2097184 | tf_op jit(solution)/shard_map/all_to_all | solution.py:155
  1431.3 32.3 %all-to-all-done.28 = f32[1,4,1,131072]{3,2,0,1:T(1,128)S(1)} async-done(((f32[1,4,1,131072]{3,2,0,1:T(1,128)}), f32[1,4,1,131072]{3,2,0,1:T(1,128)S(1)}, u32[]{:S(2)}, u32[]{:S(2)}) %all-to-all-start.28) | async-done | bytes 2097184 | tf_op jit(solution)/shard_map/all_to_all | solution.py:155
  1483.5 32.3 %all-to-all-done.17 = f32[1,4,1,131072]{3,2,0,1:T(1,128)} async-done(((f32[1,4,1,131072]{3,2,0,1:T(1,128)}), f32[1,4,1,131072]{3,2,0,1:T(1,128)}, u32[]{:S(2)}, u32[]{:S(2)}) %all-to-all-start.17) | async-done | bytes 2097184 | tf_op jit(solution)/shard_map/all_to_all | solution.py:158
  1558.3 14.0 fusion.37
  1640.4 14.0 fusion.39
  1723.0 13.7 fusion.38
  1759.5 11.6 pad_maximum_fusion.1
  1784.8 29.7 %copy.266 = f32[16,3,2,64,512]{3,1,2,0,4:T(4,128)} copy(f32[16,3,2,64,512]{4,3,2,1,0:T(8,128)} %pad_maximum_fusion.1) | data formatting | bytes 25165824 | tf_op jit(solution)/shard_map/vmap(jit(_roll_dynamic))/concatenate | solution.py:20
  1814.5 16.1 gather_fusion.1
  1830.7 14.8 copy.267
  1898.3 9.7 fusion.82
  1931.6 8.9 fusion.83
  (509 shorter events, 1367.2 us)
Async XLA Ops:
  131.4 24.0 %all-to-all-start.4 = ((f32[1,8,16,2048]{3,2,0,1:T(8,128)}), f32[1,8,16,2048]{3,2,0,1:T(8,128)}, u32[]{:S(2)}, u32[]{:S(2)}) async-start(f32[1,8,16,2048]{3,2,0,1:T(8,128)} %bitcast.769), calls=%async_computation.4 | async-start | bytes 2097152 | tf_op jit(solution)/shard_map/all_to_all | solution.py:103
  155.4 24.3 %all-to-all-start.8 = ((f32[1,8,16,2048]{3,2,0,1:T(8,128)}), f32[1,8,16,2048]{3,2,0,1:T(8,128)S(1)}, u32[]{:S(2)}, u32[]{:S(2)}) async-start(f32[1,8,16,2048]{3,2,0,1:T(8,128)} %bitcast.770), calls=%async_computation.8 | async-start | bytes 2097152 | tf_op jit(solution)/shard_map/all_to_all | solution.py:103
  180.6 24.0 %all-to-all-start.20 = ((f32[1,8,16,2048]{3,2,0,1:T(8,128)}), f32[1,8,16,2048]{3,2,0,1:T(8,128)S(1)}, u32[]{:S(2)}, u32[]{:S(2)}) async-start(f32[1,8,16,2048]{3,2,0,1:T(8,128)} %bitcast.768), calls=%async_computation.20 | async-start | bytes 2097152 | tf_op jit(solution)/shard_map/all_to_all | solution.py:103
  204.7 24.2 %all-to-all-start.12 = ((f32[1,8,16,2048]{3,2,0,1:T(8,128)}), f32[1,8,16,2048]{3,2,0,1:T(8,128)}, u32[]{:S(2)}, u32[]{:S(2)}) async-start(f32[1,8,16,2048]{3,2,0,1:T(8,128)} %bitcast.771), calls=%async_computation.12 | async-start | bytes 2097152 | tf_op jit(solution)/shard_map/all_to_all | solution.py:103
  228.9 24.0 %all-to-all-start.24 = ((f32[1,8,16,2048]{3,2,0,1:T(8,128)}), f32[1,8,16,2048]{3,2,0,1:T(8,128)}, u32[]{:S(2)}, u32[]{:S(2)}) async-start(f32[1,8,16,2048]{3,2,0,1:T(8,128)} %bitcast.766), calls=%async_computation.24 | async-start | bytes 2097152 | tf_op jit(solution)/shard_map/all_to_all | solution.py:103
  272.0 19.0 all-to-all-start.25
  291.0 19.6 all-to-all-start.1
  310.6 18.9 all-to-all-start.13
  329.5 19.6 all-to-all-start.21
  368.0 46.4 %all-to-all-start.9 = ((f32[1,8,16,2048]{3,2,0,1:T(8,128)}), f32[1,8,16,2048]{3,2,0,1:T(8,128)S(1)}, u32[]{:S(2)}, u32[]{:S(2)}) async-start(f32[1,8,16,2048]{3,2,0,1:T(8,128)} %bitcast.765), calls=%async_computation.9 | async-start | bytes 2097152 | tf_op jit(solution)/shard_map/all_to_all | solution.py:106
  415.4 50.4 %all-to-all-start.6 = ((f32[1,4,1,131072]{3,2,0,1:T(1,128)}), f32[1,4,1,131072]{3,2,0,1:T(1,128)S(1)}, u32[]{:S(2)}, u32[]{:S(2)}) async-start(f32[1,4,1,131072]{3,2,0,1:T(1,128)} %reshape_squeeze.146), calls=%async_computation.6 | async-start | bytes 4194304 | tf_op jit(solution)/shard_map/all_to_all | solution.py:127
  465.8 52.4 %all-to-all-start.7 = ((f32[1,4,1,131072]{3,2,0,1:T(1,128)}), f32[1,4,1,131072]{3,2,0,1:T(1,128)}, u32[]{:S(2)}, u32[]{:S(2)}) async-start(f32[1,4,1,131072]{3,2,0,1:T(1,128)} %reshape_squeeze.147), calls=%async_computation.7 | async-start | bytes 4194304 | tf_op jit(solution)/shard_map/all_to_all | solution.py:130
  518.2 51.8 %all-to-all-start.10 = ((f32[1,4,1,131072]{3,2,0,1:T(1,128)}), f32[1,4,1,131072]{3,2,0,1:T(1,128)S(1)}, u32[]{:S(2)}, u32[]{:S(2)}) async-start(f32[1,4,1,131072]{3,2,0,1:T(1,128)} %reshape_squeeze.148), calls=%async_computation.10 | async-start | bytes 4194304 | tf_op jit(solution)/shard_map/all_to_all | solution.py:127
  570.0 52.2 %all-to-all-start.22 = ((f32[1,4,1,131072]{3,2,0,1:T(1,128)}), f32[1,4,1,131072]{3,2,0,1:T(1,128)}, u32[]{:S(2)}, u32[]{:S(2)}) async-start(f32[1,4,1,131072]{3,2,0,1:T(1,128)} %reshape_squeeze.156), calls=%async_computation.22 | async-start | bytes 4194304 | tf_op jit(solution)/shard_map/all_to_all | solution.py:127
  622.2 51.6 %all-to-all-start.23 = ((f32[1,4,1,131072]{3,2,0,1:T(1,128)}), f32[1,4,1,131072]{3,2,0,1:T(1,128)S(1)}, u32[]{:S(2)}, u32[]{:S(2)}) async-start(f32[1,4,1,131072]{3,2,0,1:T(1,128)} %reshape_squeeze.157), calls=%async_computation.23 | async-start | bytes 4194304 | tf_op jit(solution)/shard_map/all_to_all | solution.py:130
  673.8 52.2 %all-to-all-start.14 = ((f32[1,4,1,131072]{3,2,0,1:T(1,128)}), f32[1,4,1,131072]{3,2,0,1:T(1,128)}, u32[]{:S(2)}, u32[]{:S(2)}) async-start(f32[1,4,1,131072]{3,2,0,1:T(1,128)} %reshape_squeeze.150), calls=%async_computation.14 | async-start | bytes 4194304 | tf_op jit(solution)/shard_map/all_to_all | solution.py:127
  726.0 51.8 %all-to-all-start.15 = ((f32[1,4,1,131072]{3,2,0,1:T(1,128)}), f32[1,4,1,131072]{3,2,0,1:T(1,128)S(1)}, u32[]{:S(2)}, u32[]{:S(2)}) async-start(f32[1,4,1,131072]{3,2,0,1:T(1,128)} %reshape_squeeze.151), calls=%async_computation.15 | async-start | bytes 4194304 | tf_op jit(solution)/shard_map/all_to_all | solution.py:130
  777.8 52.2 %all-to-all-start.2 = ((f32[1,4,1,131072]{3,2,0,1:T(1,128)}), f32[1,4,1,131072]{3,2,0,1:T(1,128)}, u32[]{:S(2)}, u32[]{:S(2)}) async-start(f32[1,4,1,131072]{3,2,0,1:T(1,128)} %reshape_squeeze.144), calls=%async_computation.2 | async-start | bytes 4194304 | tf_op jit(solution)/shard_map/all_to_all | solution.py:127
  830.0 51.6 %all-to-all-start.3 = ((f32[1,4,1,131072]{3,2,0,1:T(1,128)}), f32[1,4,1,131072]{3,2,0,1:T(1,128)S(1)}, u32[]{:S(2)}, u32[]{:S(2)}) async-start(f32[1,4,1,131072]{3,2,0,1:T(1,128)} %reshape_squeeze.145), calls=%async_computation.3 | async-start | bytes 4194304 | tf_op jit(solution)/shard_map/all_to_all | solution.py:130
  881.6 52.2 %all-to-all-start.26 = ((f32[1,4,1,131072]{3,2,0,1:T(1,128)}), f32[1,4,1,131072]{3,2,0,1:T(1,128)}, u32[]{:S(2)}, u32[]{:S(2)}) async-start(f32[1,4,1,131072]{3,2,0,1:T(1,128)} %reshape_squeeze.158), calls=%async_computation.26 | async-start | bytes 4194304 | tf_op jit(solution)/shard_map/all_to_all | solution.py:127
  933.8 51.4 %all-to-all-start.27 = ((f32[1,4,1,131072]{3,2,0,1:T(1,128)}), f32[1,4,1,131072]{3,2,0,1:T(1,128)S(1)}, u32[]{:S(2)}, u32[]{:S(2)}) async-start(f32[1,4,1,131072]{3,2,0,1:T(1,128)} %reshape_squeeze.159), calls=%async_computation.27 | async-start | bytes 4194304 | tf_op jit(solution)/shard_map/all_to_all | solution.py:130
  985.2 200.6 %all-to-all-start.11 = ((f32[1,4,1,131072]{3,2,0,1:T(1,128)}), f32[1,4,1,131072]{3,2,0,1:T(1,128)}, u32[]{:S(2)}, u32[]{:S(2)}) async-start(f32[1,4,1,131072]{3,2,0,1:T(1,128)} %reshape_squeeze.149), calls=%async_computation.11 | async-start | bytes 4194304 | tf_op jit(solution)/shard_map/all_to_all | solution.py:130
  1185.9 49.4 %all-to-all-start.32 = ((f32[1,4,1,131072]{3,2,0,1:T(1,128)}), f32[1,4,1,131072]{3,2,0,1:T(1,128)}, u32[]{:S(2)}, u32[]{:S(2)}) async-start(f32[1,4,1,131072]{3,2,0,1:T(1,128)} %reshape_squeeze.164), calls=%async_computation.32 | async-start | bytes 4194304 | tf_op jit(solution)/shard_map/all_to_all | solution.py:155
  1235.3 127.8 %all-to-all-start.33 = ((f32[1,4,1,131072]{3,2,0,1:T(1,128)}), f32[1,4,1,131072]{3,2,0,1:T(1,128)}, u32[]{:S(2)}, u32[]{:S(2)}) async-start(f32[1,4,1,131072]{3,2,0,1:T(1,128)} %reshape_squeeze.165), calls=%async_computation.33 | async-start | bytes 4194304 | tf_op jit(solution)/shard_map/all_to_all | solution.py:158
  1363.1 49.0 %all-to-all-start.16 = ((f32[1,4,1,131072]{3,2,0,1:T(1,128)}), f32[1,4,1,131072]{3,2,0,1:T(1,128)}, u32[]{:S(2)}, u32[]{:S(2)}) async-start(f32[1,4,1,131072]{3,2,0,1:T(1,128)} %reshape_squeeze.152), calls=%async_computation.16 | async-start | bytes 4194304 | tf_op jit(solution)/shard_map/all_to_all | solution.py:155
  1412.2 51.4 %all-to-all-start.28 = ((f32[1,4,1,131072]{3,2,0,1:T(1,128)}), f32[1,4,1,131072]{3,2,0,1:T(1,128)S(1)}, u32[]{:S(2)}, u32[]{:S(2)}) async-start(f32[1,4,1,131072]{3,2,0,1:T(1,128)} %reshape_squeeze.160), calls=%async_computation.28 | async-start | bytes 4194304 | tf_op jit(solution)/shard_map/all_to_all | solution.py:155
  1463.6 52.2 %all-to-all-start.17 = ((f32[1,4,1,131072]{3,2,0,1:T(1,128)}), f32[1,4,1,131072]{3,2,0,1:T(1,128)}, u32[]{:S(2)}, u32[]{:S(2)}) async-start(f32[1,4,1,131072]{3,2,0,1:T(1,128)} %reshape_squeeze.153), calls=%async_computation.17 | async-start | bytes 4194304 | tf_op jit(solution)/shard_map/all_to_all | solution.py:158
  1515.8 66.9 %all-to-all-start.29 = ((f32[1,4,1,131072]{3,2,0,1:T(1,128)}), f32[1,4,1,131072]{3,2,0,1:T(1,128)}, u32[]{:S(2)}, u32[]{:S(2)}) async-start(f32[1,4,1,131072]{3,2,0,1:T(1,128)} %reshape_squeeze.161), calls=%async_computation.29 | async-start | bytes 4194304 | tf_op jit(solution)/shard_map/all_to_all | solution.py:158
  1600.8 64.1 %all-to-all-start.35 = ((f32[1,8,1,32768]{3,2,0,1:T(1,128)}), f32[1,8,1,32768]{3,2,0,1:T(1,128)}, u32[]{:S(2)}, u32[]{:S(2)}) async-start(f32[1,8,1,32768]{3,2,0,1:T(1,128)} %reshape_squeeze.167), calls=%async_computation.35 | async-start | bytes 2097152 | tf_op jit(solution)/shard_map/all_to_all | solution.py:179
  1683.2 63.1 %all-to-all-start.19 = ((f32[1,8,1,32768]{3,2,0,1:T(1,128)}), f32[1,8,1,32768]{3,2,0,1:T(1,128)}, u32[]{:S(2)}, u32[]{:S(2)}) async-start(f32[1,8,1,32768]{3,2,0,1:T(1,128)} %reshape_squeeze.155), calls=%async_computation.19 | async-start | bytes 2097152 | tf_op jit(solution)/shard_map/all_to_all | solution.py:179
  1746.2 32.6 %all-to-all-start.30 = ((f32[1,8,1,32768]{3,2,0,1:T(1,128)}), f32[1,8,1,32768]{3,2,0,1:T(1,128)}, u32[]{:S(2)}, u32[]{:S(2)}) async-start(f32[1,8,1,32768]{3,2,0,1:T(1,128)} %reshape_squeeze.162), calls=%async_computation.30 | async-start | bytes 2097152 | tf_op jit(solution)/shard_map/all_to_all | solution.py:176
  1778.8 139.4 %all-to-all-start.31 = ((f32[1,8,1,32768]{3,2,0,1:T(1,128)}), f32[1,8,1,32768]{3,2,0,1:T(1,128)}, u32[]{:S(2)}, u32[]{:S(2)}) async-start(f32[1,8,1,32768]{3,2,0,1:T(1,128)} %reshape_squeeze.163), calls=%async_computation.31 | async-start | bytes 2097152 | tf_op jit(solution)/shard_map/all_to_all | solution.py:179
  (95 other events, 1288.3 us)
where the time goes:
time: 2000 us; the launch traced here: 1980 us
  local copies, waits for them, and re-layouts  914 us (46%)
  waiting for transfers between devices  374 us (19%)
  matrix products  243 us (12%)
  other arithmetic  220 us (11%)
  starting transfers between devices  216 us (11%)
    dot_general x27, matrix products, product_high(): jnp.einsum(formula, first_arg, second_arg, precision=lax.Precision.HIGHEST)  243 us
    another operation x50, local copies, waits for them, and re-layouts, rotate(): stacked = jnp.stack([real_part, imag_part])  209 us
    slice x45, local copies, waits for them, and re-layouts, rotate(): return (result[0], result[1])  185 us
    all_to_all x6, waiting for transfers between devices, to_physical(): lax.all_to_all(third_real.reshape(flat_shape), 'col', split_axis=1, conca...  167 us
    another operation x24, local copies, waits for them, and re-layouts, to_physical(): jnp.stack([fourth_real.reshape(deep_shape), fourth_imag.reshape(deep_shap...  126 us
    all_to_all x3, waiting for transfers between devices, to_spectral(): lax.all_to_all(first_real.reshape(flat_shape), 'col', split_axis=1, conca...  85.5 us
    gather x4, local copies, waits for them, and re-layouts, shift_row(): return jnp.roll(row_data, -amount_one, axis=-1)  62 us
    concatenate x2, local copies, waits for them, and re-layouts, shift_row(): return jnp.roll(row_data, -amount_one, axis=-1)  59.4 us
  transfers between devices with their start and end apart: 36, of which 23 were waited for; matrix products, arithmetic and copies ran while one was open for 60% of the time, Pallas kernels for 0%

commit v1 on v0

v1 whole, which is shorter than its diff:
```python
import jax
import jax.numpy as jnp
import numpy as np
from jax import lax
from jax.experimental import pallas as pl
from jax.experimental.pallas import tpu as pltpu
from jax.sharding import PartitionSpec as P

NX = 256
NY = 256
NZ = 256


def tables(period):
    positions = np.arange(period)
    angles = (positions[:, None] * positions[None, :] % period) * (2.0 * np.pi / period)
    factor = 1.0 / np.sqrt(period)
    return np.cos(angles) * factor, np.sin(angles) * factor


def dot(formula, first, second):
    return jnp.einsum(
        formula, first, second, precision=lax.Precision.HIGH, preferred_element_type=jnp.float32
    )


def const(table):
    return jnp.asarray(np.ascontiguousarray(table), jnp.float32)


def make_tables(half_x, rows, cols):
    cos_x, sin_x = tables(NX)
    cos_y, sin_y = tables(NY)
    cos_z, sin_z = tables(NZ)
    block_y = NY // cols
    block_z = NZ // rows
    width_z = NZ // cols
    width_x = half_x // rows
    cy = cos_y.reshape(NY, cols, 1, block_y)
    sy = sin_y.reshape(NY, cols, 1, block_y)
    inv_y = np.stack([np.concatenate([cy, sy], 2), np.concatenate([-sy, cy], 2)])
    inv_y = inv_y.reshape(2 * NY, cols, 2 * block_y)
    cz = cos_z.reshape(rows, block_z, cols, width_z)
    sz = sin_z.reshape(rows, block_z, cols, width_z)
    inv_z = np.stack([cz, sz], 2)
    weight = np.where(np.arange(half_x) == 0, 1.0, 2.0)
    inv_x = np.stack([cos_x[:, :half_x] * weight, -sin_x[:, :half_x] * weight], 1)
    cx = cos_x[:half_x].reshape(rows, width_x, NX)
    sx = sin_x[:half_x].reshape(rows, width_x, NX)
    fwd_x = np.stack([cx, -sx], 1)
    cz = cos_z.reshape(cols, width_z, rows, block_z)
    sz = sin_z.reshape(cols, width_z, rows, block_z)
    fwd_z = np.stack([cz, sz], 2)
    cy = cos_y.reshape(cols, block_y, NY)
    sy = sin_y.reshape(cols, block_y, NY)
    fwd_y = np.concatenate(
        [np.concatenate([cy, -sy], 2), np.concatenate([sy, cy], 2)], 1
    )
    return [const(table) for table in (inv_y, inv_z, inv_x, fwd_x, fwd_z, fwd_y)]


def exchange(field, axis):
    return lax.all_to_all(field, axis, split_axis=0, concat_axis=0, tiled=True)


def to_grid(smooth, inv_y, inv_z, inv_x):
    part = dot("abk,kqj->qabj", smooth, inv_y)
    part = exchange(part, "col")
    half = part.shape[-1] // 2
    turned = jnp.concatenate([-part[..., half:], part[..., :half]], -1)
    part = dot("rzuhb,uhabk->razk", inv_z, jnp.stack([part, turned]))
    part = exchange(part, "row")
    rows, width, block_z, lanes = part.shape
    part = part.reshape(rows * width, block_z, lanes)
    mid = block_z // 2
    packed = jnp.stack(
        [
            jnp.concatenate([piece[:, :mid], piece[:, mid:]], -1)
            for piece in (part[..., :half], part[..., half:])
        ]
    )
    return dot("xtk,tkmj->xmj", inv_x, packed)


def to_modes(grid, fwd_x, fwd_z, fwd_y):
    part = exchange(dot("rtax,xmj->rtamj", fwd_x, grid), "row")
    half = part.shape[-1] // 2
    part = jnp.concatenate(
        [
            jnp.concatenate([part[:, t, ..., :half], part[:, t, ..., half:]], 2)
            for t in range(2)
        ],
        -1,
    )
    turned = jnp.concatenate([part[..., half:], -part[..., :half]], -1)
    part = dot("qbuhz,uhazk->qabk", fwd_z, jnp.stack([part, turned]))
    part = exchange(part, "col")
    return dot("habk,hkj->abj", part, fwd_y)


def geometry(base, real, shape):
    index_x = base[0] + pl.program_id(0)
    kx = index_x.astype(jnp.float32)
    iz = lax.broadcasted_iota(jnp.int32, shape, 0) + base[1]
    iz = jnp.where(2 * iz < NZ, iz, iz - NZ)
    iy = lax.broadcasted_iota(jnp.int32, shape, 1)
    iy = jnp.where(2 * iy < NY, iy, iy - NY)
    k0 = jnp.full(shape, kx, jnp.float32)
    k1 = iy.astype(jnp.float32) - real[4] * k0
    k2 = iz.astype(jnp.float32)
    ksq = k0 * k0 + k1 * k1 + k2 * k2
    inv = 1.0 / jnp.maximum(ksq, 1.0)
    keep = (3 * jnp.abs(iz) < NZ) & (3 * jnp.abs(iy) < NY) & (3.0 * k0 < float(NX))
    mask = jnp.where(keep, 1.0, 0.0)
    return (k0, k1, k2), ksq, inv, mask


def project(field, k, inv):
    along = (k[0] * field[0] + k[1] * field[1] + k[2] * field[2]) * inv
    return [field[c] - k[c] * along for c in range(3)]


def first_kernel(amount, base, real, vel, smooth, sums):
    shape = vel.shape[3:]
    full_y = shape[1]
    k, ksq, inv, mask = geometry(base, real, shape)
    shift = amount[pl.program_id(0)]
    v = [[pltpu.roll(vel[c, p, 0], shift, 1) for p in range(2)] for c in range(3)]
    stress = v[0][0] * v[1][0] + v[0][1] * v[1][1]
    energy = sum(v[c][p] * v[c][p] for c in range(3) for p in range(2))
    sums[0, 0:1] = jnp.sum(stress, axis=0, keepdims=True)
    sums[0, 1:2] = jnp.sum(ksq * energy, axis=0, keepdims=True)
    for p in range(2):
        out = project([v[c][p] for c in range(3)], k, inv)
        for c in range(3):
            smooth[c, 0, :, p * full_y : (p + 1) * full_y] = mask * out[c]


def last_kernel(amount, base, real, vel, acc, d0, d1, t01, t02, t12, new_vel, new_acc):
    shape = vel.shape[3:]
    full_y = shape[1]
    k, ksq, inv, mask = geometry(base, real, shape)
    shift = amount[pl.program_id(0)]
    viscosity, shear, step = real[0], real[1], real[3]
    coupling = 2.0 * shear * k[0] * inv
    for p in range(2):
        v = [pltpu.roll(vel[c, p, 0], shift, 1) for c in range(3)]
        old = [pltpu.roll(acc[c, p, 0], shift, 1) for c in range(3)]
        sign = mask if p == 0 else -mask
        other = slice((1 - p) * full_y, (2 - p) * full_y)
        e0, e1, e01, e02, e12 = [ref[0, :, other] for ref in (d0, d1, t01, t02, t12)]
        hat = [
            sign * (k[0] * e0 + k[1] * e01 + k[2] * e02),
            sign * (k[0] * e01 + k[1] * e1 + k[2] * e12),
            sign * (k[0] * e02 + k[1] * e12),
        ]
        hat = project(hat, k, inv)
        for c in range(3):
            rate = hat[c] + coupling * k[c] * v[1] - viscosity * ksq * v[c]
            if c == 0:
                rate = rate - shear * v[1]
            total = (-5.0 / 9.0) * old[c] + step * rate
            new_acc[c, p, 0] = total
            new_vel[c, p, 0] = v[c] + (15.0 / 16.0) * total


def body(velocity, accumulator, remesh_flag, remesh_shift, viscosity, shear, clock, step):
    rows = lax.axis_size("row")
    cols = lax.axis_size("col")
    _, _, width_x, width_z, full_y = velocity.shape
    amount = jnp.mod(-(remesh_flag * remesh_shift), full_y).astype(jnp.int32)
    base = jnp.stack(
        [lax.axis_index("row") * width_x, lax.axis_index("col") * width_z]
    ).astype(jnp.int32)
    real = jnp.concatenate([viscosity, shear, clock, step, shear * clock])
    state_spec = pl.BlockSpec((3, 2, 1, width_z, full_y), lambda i, *_: (0, 0, i, 0, 0))
    mode_spec = pl.BlockSpec((1, width_z, 2 * full_y), lambda i, *_: (i, 0, 0))
    params = pltpu.CompilerParams(
        dimension_semantics=("arbitrary",), vmem_limit_bytes=48 * 1024 * 1024
    )
    smooth, sums = pl.pallas_call(
        first_kernel,
        grid_spec=pltpu.PrefetchScalarGridSpec(
            num_scalar_prefetch=3,
            grid=(width_x,),
            in_specs=[state_spec],
            out_specs=[
                pl.BlockSpec((3, 1, width_z, 2 * full_y), lambda i, *_: (0, i, 0, 0)),
                pl.BlockSpec((1, 2, full_y), lambda i, *_: (i, 0, 0)),
            ],
        ),
        out_shape=[
            jax.ShapeDtypeStruct((3, width_x, width_z, 2 * full_y), jnp.float32),
            jax.ShapeDtypeStruct((width_x, 2, full_y), jnp.float32),
        ],
        compiler_params=params,
    )(amount, base, real, velocity)
    totals = lax.psum(jnp.sum(sums, axis=-1), "col")
    inv_y, inv_z, inv_x, fwd_x, fwd_z, fwd_y = make_tables(width_x * rows, rows, cols)
    u, v, w = [to_grid(smooth[c], inv_y, inv_z, inv_x) for c in range(3)]
    products = (u * u - w * w, v * v - w * w, u * v, u * w, v * w)
    modes = [to_modes(product, fwd_x, fwd_z, fwd_y) for product in products]
    new_velocity, new_accumulator = pl.pallas_call(
        last_kernel,
        grid_spec=pltpu.PrefetchScalarGridSpec(
            num_scalar_prefetch=3,
            grid=(width_x,),
            in_specs=[state_spec] * 2 + [mode_spec] * 5,
            out_specs=[state_spec] * 2,
        ),
        out_shape=[jax.ShapeDtypeStruct(velocity.shape, jnp.float32)] * 2,
        compiler_params=params,
    )(amount, base, real, velocity, accumulator, *modes)
    stress = totals[:, 0] / (NY * NZ)
    dissipation = 2.0 * viscosity[0] * totals[:, 1] / (NY * NZ)
    return new_velocity, new_accumulator, jnp.stack([stress, dissipation])


def solution(mesh):
    state = P(None, None, "row", "col", None)
    in_specs = (state, state, P("row"), P("row"), P(), P(), P(), P())
    out_specs = (state, state, P(None, "row"))
    return jax.shard_map(
        body, mesh=mesh, in_specs=in_specs, out_specs=out_specs, check_vma=False
    )
```

time: 2000 us -> 744 us (0.37)
  local copies, waits for them, and re-layouts: 914 us -> 69.8 us
  other arithmetic: 220 us -> 18.2 us
  matrix products: 243 us -> 77.3 us
  starting transfers between devices: 216 us -> 102 us
  blocking collectives: 8.85 us -> 49 us
  Pallas kernels: 0 us -> 31.9 us
    another operation x112 -> x0, local copies, waits for them, and re-layouts: 516 us -> none  [the longest x50 209 us: rotate(): stacked = jnp.stack([real_part, imag_part])]
    slice x56 -> x3, local copies, waits for them, and re-layouts: 229 us -> 10.8 us  [to_grid(): piece[:, :mid]]
    dot_general x27 -> x24, matrix products: 243 us -> 77.3 us  [dot(): jnp.einsum(formula, first, second, precision=lax.Precision.HIGH, preferre...]
    all_to_all x24 -> x0, other arithmetic: 156 us -> none  [the longest x6 45.1 us: to_physical(): lax.all_to_all(third_imag.reshape(flat_shape), 'col', split_axis=1, conca...]
    all_to_all x36 -> x16, starting transfers between devices: 216 us -> 102 us  [exchange(): return lax.all_to_all(field, axis, split_axis=0, concat_axis=0, tiled=True)]
    gather x4 -> x0, local copies, waits for them, and re-layouts: 62 us -> none  [shift_row(): return jnp.roll(row_data, -amount_one, axis=-1)]
    concatenate x2 -> x1, local copies, waits for them, and re-layouts: 59.4 us -> 0.08 us  [body(): real = jnp.concatenate([viscosity, shear, clock, step, shear * clock])]
    psum x1, blocking collectives: 8.85 us -> 49 us  [body(): totals = lax.psum(jnp.sum(sums, axis=-1), 'col')]
  transfers between devices with their start and end apart: 36 -> 16, of which waited for: 23 -> 14; matrix products, arithmetic and copies ran while one was open for 60% -> 20% of each run, Pallas kernels for 0% -> 0%
where the time goes in v1:
time: 744 us; the launch traced here: 734 us
  waiting for transfers between devices  382 us (51%)
  starting transfers between devices  102 us (14%)
  matrix products  77.3 us (10%)
  local copies, waits for them, and re-layouts  69.8 us (9%)
  blocking collectives  49 us (7%)
  Pallas kernels  31.9 us (4%)
  other arithmetic  18.2 us (2%)
    all_to_all x16, waiting for transfers between devices, exchange(): return lax.all_to_all(field, axis, split_axis=0, concat_axis=0, tiled=True)  382 us
    all_to_all x16, starting transfers between devices, exchange(): return lax.all_to_all(field, axis, split_axis=0, concat_axis=0, tiled=True)  102 us
    dot_general x24, matrix products, dot(): jnp.einsum(formula, first, second, precision=lax.Precision.HIGH, preferre...  77.3 us
    psum x1, blocking collectives, body(): totals = lax.psum(jnp.sum(sums, axis=-1), 'col')  49 us
    unnamed x54, local copies, waits for them, and re-layouts  29.3 us
    pallas_call x1, Pallas kernels, body(): pl.pallas_call(last_kernel, grid_spec=pltpu.PrefetchScalarGridSpec(num_sc...  18.8 us
  transfers between devices with their start and end apart: 16, of which 14 were waited for; matrix products, arithmetic and copies ran while one was open for 20% of the time, Pallas kernels for 0%

profile of v1, /device:TPU:18, one launch (start us, length us, event | category | flops | bytes accessed | tf_op | source)
XLA Modules:
  0.0 733.9 jit_solution(17298831703352190883)
XLA Ops:
  4.1 13.1 %shard_map.157 = (f32[3,16,64,512]{3,2,1,0:T(8,128)}, f32[16,2,256]{2,1,0:T(2,128)S(1)}) custom-call(s32[16]{0:T(128)S(1)} %and_select_fusion.amount, s32[2]{0:T(128)S(1)} %pad_add_fusion.base, f32[5]{0:T(128)S(1)} %concatenate.90.real, f32[3,2,16,64,256]{4,3,2,1,0:T(8,128)} %vel.3), custom_call_target="tpu_custom_call" | custom-call | tf_op jit(solution)/shard_map/pallas_call | solution.py:181
  22.1 5.2 all-to-all-start.6
  32.2 40.0 %all-to-all-done.6 = f32[4,16,64,128]{3,2,1,0:T(8,128)S(1)} async-done(((f32[4,16,64,128]{3,2,1,0:T(8,128)}), f32[4,16,64,128]{3,2,1,0:T(8,128)S(1)}, u32[]{:S(2)}, u32[]{:S(2)}) %all-to-all-start.6) | async-done | bytes 2097184 | tf_op jit(solution)/shard_map/all_to_all | solution.py:63
  73.6 7.7 %all-to-all-start = ((f32[4,16,64,128]{3,2,1,0:T(8,128)}), f32[4,16,64,128]{3,2,1,0:T(8,128)}, u32[]{:S(2)}, u32[]{:S(2)}) async-start(f32[4,16,64,128]{3,2,1,0:T(8,128)} %copy.140), calls=%async_computation | async-start | bytes 4194304 | tf_op jit(solution)/shard_map/all_to_all | solution.py:63
  86.2 39.5 %all-to-all-done = f32[4,16,64,128]{3,2,1,0:T(8,128)} async-done(((f32[4,16,64,128]{3,2,1,0:T(8,128)}), f32[4,16,64,128]{3,2,1,0:T(8,128)}, u32[]{:S(2)}, u32[]{:S(2)}) %all-to-all-start) | async-done | bytes 2097184 | tf_op jit(solution)/shard_map/all_to_all | solution.py:63
  125.8 7.0 all-to-all-start.2
  139.9 37.4 %all-to-all-done.2 = f32[4,16,64,128]{3,2,1,0:T(8,128)S(1)} async-done(((f32[4,16,64,128]{3,2,1,0:T(8,128)}), f32[4,16,64,128]{3,2,1,0:T(8,128)S(1)}, u32[]{:S(2)}, u32[]{:S(2)}) %all-to-all-start.2) | async-done | bytes 2097184 | tf_op jit(solution)/shard_map/all_to_all | solution.py:63
  189.5 18.5 %all-to-all-done.1 = f32[8,16,32,128]{3,2,1,0:T(8,128)S(1)} async-done(((f32[8,16,32,128]{3,2,1,0:T(8,128)}), f32[8,16,32,128]{3,2,1,0:T(8,128)S(1)}, u32[]{:S(2)}, u32[]{:S(2)}) %all-to-all-start.1) | async-done | bytes 2097184 | tf_op jit(solution)/shard_map/all_to_all | solution.py:63
  208.1 5.8 all-to-all-start.3
  220.4 18.7 %all-to-all-done.3 = f32[8,16,32,128]{3,2,1,0:T(8,128)} async-done(((f32[8,16,32,128]{3,2,1,0:T(8,128)}), f32[8,16,32,128]{3,2,1,0:T(8,128)}, u32[]{:S(2)}, u32[]{:S(2)}) %all-to-all-start.3) | async-done | bytes 2097184 | tf_op jit(solution)/shard_map/all_to_all | solution.py:63
  239.0 6.0 all-to-all-start.7
  280.1 21.1 %all-to-all-done.12 = f32[8,2,16,16,128]{4,2,3,1,0:T(8,128)} async-done(((f32[8,2,16,16,128]{4,2,3,1,0:T(8,128)}), f32[8,2,16,16,128]{4,2,3,1,0:T(8,128)}, u32[]{:S(2)}, u32[]{:S(2)}) %all-to-all-start.12) | async-done | bytes 2097184 | tf_op jit(solution)/shard_map/all_to_all | solution.py:63
  301.3 6.1 all-to-all-start.4
  327.0 5.5 all-to-all-done.4
  332.6 5.8 all-to-all-start.10
  342.4 21.2 %all-to-all-done.10 = f32[8,2,16,16,128]{4,2,3,1,0:T(8,128)} async-done(((f32[8,2,16,16,128]{4,2,3,1,0:T(8,128)}), f32[8,2,16,16,128]{4,2,3,1,0:T(8,128)}, u32[]{:S(2)}, u32[]{:S(2)}) %all-to-all-start.10) | async-done | bytes 2097184 | tf_op jit(solution)/shard_map/all_to_all | solution.py:63
  363.5 5.8 all-to-all-start.8
  373.3 21.2 %all-to-all-done.8 = f32[8,2,16,16,128]{4,2,3,1,0:T(8,128)} async-done(((f32[8,2,16,16,128]{4,2,3,1,0:T(8,128)}), f32[8,2,16,16,128]{4,2,3,1,0:T(8,128)}, u32[]{:S(2)}, u32[]{:S(2)}) %all-to-all-start.8) | async-done | bytes 2097184 | tf_op jit(solution)/shard_map/all_to_all | solution.py:63
  394.5 5.5 all-to-all-start.14
  410.3 14.9 %all-to-all-done.14 = f32[8,2,16,16,128]{4,2,3,1,0:T(8,128)S(1)} async-done(((f32[8,2,16,16,128]{4,2,3,1,0:T(8,128)}), f32[8,2,16,16,128]{4,2,3,1,0:T(8,128)S(1)}, u32[]{:S(2)}, u32[]{:S(2)}) %all-to-all-start.14) | async-done | bytes 2097184 | tf_op jit(solution)/shard_map/all_to_all | solution.py:63
  425.2 7.7 %all-to-all-start.5 = ((f32[4,16,64,128]{3,2,1,0:T(8,128)}), f32[4,16,64,128]{3,2,1,0:T(8,128)}, u32[]{:S(2)}, u32[]{:S(2)}) async-start(f32[4,16,64,128]{3,2,1,0:T(8,128)} %copy.163), calls=%async_computation.5 | async-start | bytes 4194304 | tf_op jit(solution)/shard_map/all_to_all | solution.py:63
  442.1 36.2 %all-to-all-done.5 = f32[4,16,64,128]{3,2,1,0:T(8,128)} async-done(((f32[4,16,64,128]{3,2,1,0:T(8,128)}), f32[4,16,64,128]{3,2,1,0:T(8,128)}, u32[]{:S(2)}, u32[]{:S(2)}) %all-to-all-start.5) | async-done | bytes 2097184 | tf_op jit(solution)/shard_map/all_to_all | solution.py:63
  478.3 8.0 %all-to-all-start.13 = ((f32[4,16,64,128]{3,2,1,0:T(8,128)}), f32[4,16,64,128]{3,2,1,0:T(8,128)}, u32[]{:S(2)}, u32[]{:S(2)}) async-start(f32[4,16,64,128]{3,2,1,0:T(8,128)} %copy.190), calls=%async_computation.13 | async-start | bytes 4194304 | tf_op jit(solution)/shard_map/all_to_all | solution.py:63
  493.4 37.5 %all-to-all-done.13 = f32[4,16,64,128]{3,2,1,0:T(8,128)} async-done(((f32[4,16,64,128]{3,2,1,0:T(8,128)}), f32[4,16,64,128]{3,2,1,0:T(8,128)}, u32[]{:S(2)}, u32[]{:S(2)}) %all-to-all-start.13) | async-done | bytes 2097184 | tf_op jit(solution)/shard_map/all_to_all | solution.py:63
  530.8 7.0 all-to-all-start.15
  547.1 35.2 %all-to-all-done.15 = f32[4,16,64,128]{3,2,1,0:T(8,128)S(1)} async-done(((f32[4,16,64,128]{3,2,1,0:T(8,128)}), f32[4,16,64,128]{3,2,1,0:T(8,128)S(1)}, u32[]{:S(2)}, u32[]{:S(2)}) %all-to-all-start.15) | async-done | bytes 2097184 | tf_op jit(solution)/shard_map/all_to_all | solution.py:63
  583.6 7.9 %all-to-all-start.9 = ((f32[4,16,64,128]{3,2,1,0:T(8,128)}), f32[4,16,64,128]{3,2,1,0:T(8,128)}, u32[]{:S(2)}, u32[]{:S(2)}) async-start(f32[4,16,64,128]{3,2,1,0:T(8,128)} %copy.178), calls=%async_computation.9 | async-start | bytes 4194304 | tf_op jit(solution)/shard_map/all_to_all | solution.py:63
  600.8 35.2 %all-to-all-done.9 = f32[4,16,64,128]{3,2,1,0:T(8,128)} async-done(((f32[4,16,64,128]{3,2,1,0:T(8,128)}), f32[4,16,64,128]{3,2,1,0:T(8,128)}, u32[]{:S(2)}, u32[]{:S(2)}) %all-to-all-start.9) | async-done | bytes 2097184 | tf_op jit(solution)/shard_map/all_to_all | solution.py:63
  635.9 7.8 %all-to-all-start.11 = ((f32[4,16,64,128]{3,2,1,0:T(8,128)}), f32[4,16,64,128]{3,2,1,0:T(8,128)}, u32[]{:S(2)}, u32[]{:S(2)}) async-start(f32[4,16,64,128]{3,2,1,0:T(8,128)} %copy.184), calls=%async_computation.11 | async-start | bytes 4194304 | tf_op jit(solution)/shard_map/all_to_all | solution.py:63
  643.8 49.0 %psum.7 = f32[16,2]{1,0:T(8,128)S(1)} all-reduce(f32[16,2]{1,0:T(8,128)S(1)} %reduce_sum.9), channel_id=1, replica_groups=mesh['row'=8,'col'=4] {'col'}, use_global_device_ids=true, to_apply=%region_1.2 | all-reduce | flops 32 | bytes 256 | tf_op jit(solution)/shard_map/psum | solution.py:198
  710.0 5.0 convolution_bitcast_fusion.2.t01
  715.0 18.8 %shard_map.158 = (f32[3,2,16,64,256]{4,3,2,1,0:T(8,128)}, f32[3,2,16,64,256]{4,3,2,1,0:T(8,128)}) custom-call(s32[16]{0:T(128)S(1)} %and_select_fusion.amount, s32[2]{0:T(128)S(1)} %pad_add_fusion.base, f32[5]{0:T(128)S(1)} %concatenate.90.real, f32[3,2,16,64,256]{4,3,2,1,0:T(8,128)} %vel.3, f32[3,2,16,64,256]{4,3,2,1,0:T(8,128)} %acc.1, ...), custom_call_target="tpu_custom_call" | custom-call | tf_op jit(solution)/shard_map/pallas_call | solution.py:203
  (130 shorter events, 169.1 us)
Async XLA Ops:
  4.1 13.1 %copy-start.7 = (f32[512,4,128,1]{2,0,1,3:T(8,128)S(1)}, f32[512,4,128,1]{2,0,1,3:T(8,128)}, u32[]{:S(2)}) copy-start(f32[512,4,128,1]{2,0,1,3:T(8,128)} %constant.56) | copy-start | bytes 3145732
  22.1 50.1 %all-to-all-start.6 = ((f32[4,16,64,128]{3,2,1,0:T(8,128)}), f32[4,16,64,128]{3,2,1,0:T(8,128)S(1)}, u32[]{:S(2)}, u32[]{:S(2)}) async-start(f32[4,16,64,128]{3,2,1,0:T(8,128)} %copy.164), calls=%async_computation.6 | async-start | bytes 4194304 | tf_op jit(solution)/shard_map/all_to_all | solution.py:63
  72.3 1.4 copy-start.10
  73.6 52.2 %all-to-all-start = ((f32[4,16,64,128]{3,2,1,0:T(8,128)}), f32[4,16,64,128]{3,2,1,0:T(8,128)}, u32[]{:S(2)}, u32[]{:S(2)}) async-start(f32[4,16,64,128]{3,2,1,0:T(8,128)} %copy.140), calls=%async_computation | async-start | bytes 4194304 | tf_op jit(solution)/shard_map/all_to_all | solution.py:63
  125.8 51.4 %all-to-all-start.2 = ((f32[4,16,64,128]{3,2,1,0:T(8,128)}), f32[4,16,64,128]{3,2,1,0:T(8,128)S(1)}, u32[]{:S(2)}, u32[]{:S(2)}) async-start(f32[4,16,64,128]{3,2,1,0:T(8,128)} %copy.149), calls=%async_computation.2 | async-start | bytes 4194304 | tf_op jit(solution)/shard_map/all_to_all | solution.py:63
  177.2 1.3 copy-start.11
  178.5 29.5 %all-to-all-start.1 = ((f32[8,16,32,128]{3,2,1,0:T(8,128)}), f32[8,16,32,128]{3,2,1,0:T(8,128)S(1)}, u32[]{:S(2)}, u32[]{:S(2)}) async-start(f32[8,16,32,128]{3,2,1,0:T(8,128)} %fusion.83), calls=%async_computation.1 | async-start | bytes 4194304 | tf_op jit(solution)/shard_map/all_to_all | solution.py:63
  208.1 31.0 %all-to-all-start.3 = ((f32[8,16,32,128]{3,2,1,0:T(8,128)}), f32[8,16,32,128]{3,2,1,0:T(8,128)}, u32[]{:S(2)}, u32[]{:S(2)}) async-start(f32[8,16,32,128]{3,2,1,0:T(8,128)} %fusion.82), calls=%async_computation.3 | async-start | bytes 4194304 | tf_op jit(solution)/shard_map/all_to_all | solution.py:63
  239.0 32.7 %all-to-all-start.7 = ((f32[8,16,32,128]{3,2,1,0:T(8,128)}), f32[8,16,32,128]{3,2,1,0:T(8,128)}, u32[]{:S(2)}, u32[]{:S(2)}) async-start(f32[8,16,32,128]{3,2,1,0:T(8,128)} %fusion.81), calls=%async_computation.7 | async-start | bytes 4194304 | tf_op jit(solution)/shard_map/all_to_all | solution.py:63
  247.4 5.0 copy-start.13
  262.6 1.7 copy-start.16
  262.6 1.7 copy-start.17
  264.3 1.5 copy-start.18
  264.3 1.5 copy-start.19
  264.3 1.7 copy-start.20
  268.0 1.3 copy-start.2
  271.8 29.5 %all-to-all-start.12 = ((f32[8,2,16,16,128]{4,2,3,1,0:T(8,128)}), f32[8,2,16,16,128]{4,2,3,1,0:T(8,128)}, u32[]{:S(2)}, u32[]{:S(2)}) async-start(f32[8,2,16,16,128]{4,2,3,1,0:T(8,128)} %fusion.33), calls=%async_computation.12 | async-start | bytes 4194304 | tf_op jit(solution)/shard_map/all_to_all | solution.py:63
  301.3 31.3 %all-to-all-start.4 = ((f32[8,2,16,16,128]{4,2,3,1,0:T(8,128)}), f32[8,2,16,16,128]{4,2,3,1,0:T(8,128)}, u32[]{:S(2)}, u32[]{:S(2)}) async-start(f32[8,2,16,16,128]{4,2,3,1,0:T(8,128)} %fusion.41), calls=%async_computation.4 | async-start | bytes 4194304 | tf_op jit(solution)/shard_map/all_to_all | solution.py:63
  320.5 1.7 copy-start.15
  322.2 2.4 copy-start.3
  323.3 1.3 copy-start.4
  332.6 31.0 %all-to-all-start.10 = ((f32[8,2,16,16,128]{4,2,3,1,0:T(8,128)}), f32[8,2,16,16,128]{4,2,3,1,0:T(8,128)}, u32[]{:S(2)}, u32[]{:S(2)}) async-start(f32[8,2,16,16,128]{4,2,3,1,0:T(8,128)} %fusion.35), calls=%async_computation.10 | async-start | bytes 4194304 | tf_op jit(solution)/shard_map/all_to_all | solution.py:63
  363.5 31.0 %all-to-all-start.8 = ((f32[8,2,16,16,128]{4,2,3,1,0:T(8,128)}), f32[8,2,16,16,128]{4,2,3,1,0:T(8,128)}, u32[]{:S(2)}, u32[]{:S(2)}) async-start(f32[8,2,16,16,128]{4,2,3,1,0:T(8,128)} %fusion.37), calls=%async_computation.8 | async-start | bytes 4194304 | tf_op jit(solution)/shard_map/all_to_all | solution.py:63
  394.5 30.6 %all-to-all-start.14 = ((f32[8,2,16,16,128]{4,2,3,1,0:T(8,128)}), f32[8,2,16,16,128]{4,2,3,1,0:T(8,128)S(1)}, u32[]{:S(2)}, u32[]{:S(2)}) async-start(f32[8,2,16,16,128]{4,2,3,1,0:T(8,128)} %fusion.31), calls=%async_computation.14 | async-start | bytes 4194304 | tf_op jit(solution)/shard_map/all_to_all | solution.py:63
  425.2 53.1 %all-to-all-start.5 = ((f32[4,16,64,128]{3,2,1,0:T(8,128)}), f32[4,16,64,128]{3,2,1,0:T(8,128)}, u32[]{:S(2)}, u32[]{:S(2)}) async-start(f32[4,16,64,128]{3,2,1,0:T(8,128)} %copy.163), calls=%async_computation.5 | async-start | bytes 4194304 | tf_op jit(solution)/shard_map/all_to_all | solution.py:63
  478.3 52.6 %all-to-all-start.13 = ((f32[4,16,64,128]{3,2,1,0:T(8,128)}), f32[4,16,64,128]{3,2,1,0:T(8,128)}, u32[]{:S(2)}, u32[]{:S(2)}) async-start(f32[4,16,64,128]{3,2,1,0:T(8,128)} %copy.190), calls=%async_computation.13 | async-start | bytes 4194304 | tf_op jit(solution)/shard_map/all_to_all | solution.py:63
  530.8 51.4 %all-to-all-start.15 = ((f32[4,16,64,128]{3,2,1,0:T(8,128)}), f32[4,16,64,128]{3,2,1,0:T(8,128)S(1)}, u32[]{:S(2)}, u32[]{:S(2)}) async-start(f32[4,16,64,128]{3,2,1,0:T(8,128)} %copy.196), calls=%async_computation.15 | async-start | bytes 4194304 | tf_op jit(solution)/shard_map/all_to_all | solution.py:63
  583.6 52.4 %all-to-all-start.9 = ((f32[4,16,64,128]{3,2,1,0:T(8,128)}), f32[4,16,64,128]{3,2,1,0:T(8,128)}, u32[]{:S(2)}, u32[]{:S(2)}) async-start(f32[4,16,64,128]{3,2,1,0:T(8,128)} %copy.178), calls=%async_computation.9 | async-start | bytes 4194304 | tf_op jit(solution)/shard_map/all_to_all | solution.py:63
  600.8 92.8 %copy-start.5 = (f32[4,128,512,1]{2,1,3,0:T(8,128)S(1)}, f32[4,128,512,1]{2,1,3,0:T(8,128)}, u32[]{:S(2)}) copy-start(f32[4,128,512,1]{2,1,3,0:T(8,128)} %constant.60) | copy-start | bytes 3145732
  635.9 74.0 %all-to-all-start.11 = ((f32[4,16,64,128]{3,2,1,0:T(8,128)}), f32[4,16,64,128]{3,2,1,0:T(8,128)}, u32[]{:S(2)}, u32[]{:S(2)}) async-start(f32[4,16,64,128]{3,2,1,0:T(8,128)} %copy.184), calls=%async_computation.11 | async-start | bytes 4194304 | tf_op jit(solution)/shard_map/all_to_all | solution.py:63
  697.0 5.0 copy-start.9
  710.0 5.0 copy-start
  (5 other events, 6.0 us)
